TPU v7x, 256 devices: a whole 4x4x8 slice. The times are simulated.
256 devices in a mesh: dp: 8 (over x, core), shard: 32 (over z, y).
Axes of the slice: x: 4, y: 4, z: 8, core: 2. Of those that a mesh axis runs over, the one named last changes fastest.
Arguments:
- table: float32 [65536, 128], P('shard'), may hold values from -6 to 6
- cross_weight: bfloat16 [1024, 1024], replicated, may hold values from -0.1875 to 0.1875
- cross_bias: float32 [1024], replicated, may hold values from -3 to 3
- top_weight: bfloat16 [1024, 512], replicated, may hold values from -0.1875 to 0.1875
- top_bias: float32 [512], replicated, may hold values from -3 to 3
- out_weight: float32 [512], replicated, may hold values from -0.25 to 0.25
- wanted: int32 [256, 32, 128], P(('dp', 'shard')), may hold values from 0 to 2047, as said below
- slots: int32 [131072, 8, 4], P(('dp', 'shard')), may hold values from 0 to 4095
- lengths: int32 [131072, 8], P(('dp', 'shard')), may hold values from 1 to 4
- logit_grad: float32 [131072], P(('dp', 'shard')), may hold values from -6 to 6
Outputs:
- logits: float32 [131072], P(('dp', 'shard'))
- grad_cross: float32 [1024, 1024], replicated
- grad_top: float32 [1024, 512], replicated
- grad_cross_bias: float32 [1024], replicated
- grad_top_bias: float32 [512], replicated
- grad_out: float32 [512], replicated
- table_grad: float32 [65536, 128], P('shard')
Inputs may be any that keep to these rules, and one draw needn't show every extreme that they name: `wanted`: the 128 rows that one device fetches from one owner are distinct.
All inputs are finite; a program needn't handle non-finite values.
Results may differ from a plain program's by a relative error of at most 0.0084.
Values sent between devices are 32-bit elements; how exact they have to be, the bound alone decides.
A program may use at most 128 MiB of HBM per device.

v0:
```python
import jax
import jax.numpy as jnp
from jax import lax
from jax.sharding import PartitionSpec as P


def on_device(
    table,
    cross_weight,
    cross_bias,
    top_weight,
    top_bias,
    out_weight,
    wanted,
    slots,
    lengths,
    logit_grad,
):
    emb = table.shape[1]
    samples = slots.shape[0]
    feats = slots.shape[1]
    bag = slots.shape[2]
    requests = wanted[0]
    served = lax.all_to_all(requests, "shard", split_axis=0, concat_axis=0, tiled=True)
    cache = lax.all_to_all(
        jnp.take(table, served, axis=0), "shard", split_axis=0, concat_axis=0, tiled=True
    )
    cache_flat = cache.reshape(-1, emb)
    live = (jnp.arange(bag, dtype=jnp.int32)[None, None, :] < lengths[:, :, None]).astype(
        jnp.float32
    )
    gathered = cache_flat[slots]
    pooled = jnp.sum(gathered * live[..., None], axis=2)
    x0 = pooled.reshape(samples, feats * emb).astype(jnp.bfloat16)
    xfull = x0.astype(jnp.float32)
    yval = jnp.dot(x0, cross_weight, preferred_element_type=jnp.float32) + cross_bias
    hidden = (xfull * yval + xfull).astype(jnp.bfloat16)
    zval = jnp.dot(hidden, top_weight, preferred_element_type=jnp.float32) + top_bias
    sig = jax.nn.sigmoid(zval)
    uval = zval * sig
    logits = jnp.dot(uval, out_weight, precision=lax.Precision.HIGHEST)
    g_out = jnp.dot(logit_grad, uval, precision=lax.Precision.HIGHEST)
    dz = logit_grad[:, None] * out_weight[None, :] * (sig * (1.0 + zval * (1.0 - sig)))
    dzb = dz.astype(jnp.bfloat16)
    g_top = jnp.dot(hidden.T, dzb, preferred_element_type=jnp.float32)
    g_tbias = jnp.sum(dz, axis=0)
    dh = jnp.dot(dzb, top_weight.T, preferred_element_type=jnp.float32)
    dy = dh * xfull
    dyb = dy.astype(jnp.bfloat16)
    g_cross = jnp.dot(x0.T, dyb, preferred_element_type=jnp.float32)
    g_cbias = jnp.sum(dy, axis=0)
    dx = dh * (yval + 1.0) + jnp.dot(dyb, cross_weight.T, preferred_element_type=jnp.float32)
    contrib = dx.reshape(samples, feats, 1, emb) * live[..., None]
    slot_grads = (
        jnp.zeros(cache_flat.shape, jnp.float32).at[slots.reshape(-1)].add(contrib.reshape(-1, emb))
    )
    returned = lax.all_to_all(
        slot_grads.reshape(cache.shape), "shard", split_axis=0, concat_axis=0, tiled=True
    )
    owner_grad = (
        jnp.zeros(table.shape, jnp.float32).at[served.reshape(-1)].add(returned.reshape(-1, emb))
    )
    table_grad = lax.psum(owner_grad, "dp")
    summed = lax.psum((g_cross, g_top, g_cbias, g_tbias, g_out), ("dp", "shard"))
    return (logits, summed[0], summed[1], summed[2], summed[3], summed[4], table_grad)


def solution(mesh):
    placed = (
        P("shard", None),
        P(),
        P(),
        P(),
        P(),
        P(),
        P(("dp", "shard"), None, None),
        P(("dp", "shard"), None, None),
        P(("dp", "shard"), None),
        P(("dp", "shard")),
    )
    return jax.shard_map(
        on_device,
        mesh=mesh,
        in_specs=placed,
        out_specs=(P(("dp", "shard")), P(), P(), P(), P(), P(), P("shard", None)),
        check_vma=False,
    )
```

profile of v0, /device:TPU:8, one launch (start us, length us, event | category | flops | bytes accessed | tf_op | source)
XLA Modules:
  0.0 660.7 jit_solution(8032694361163079819)
XLA Ops:
  7.2 0.0 copy-start
  7.2 0.0 copy-start.1
  7.2 12.0 %all-to-all-start = ((s32[32,1,128]{2,1,0:T(1,128)}), s32[32,1,128]{2,1,0:T(1,128)S(1)}, u32[]{:S(2)}, u32[]{:S(2)}) async-start(s32[32,1,128]{2,1,0:T(1,128)} %bitcast.60), calls=%async_computation | async-start | bytes 32768 | tf_op jit(solution)/shard_map/all_to_all | solution.py:24
  19.2 0.8 copy.22
  20.0 2.6 fusion.4
  22.6 5.0 all-to-all-done
  27.7 0.0 copy-done.1
  27.7 14.2 %gather_fusion = f32[4096,128]{1,0:T(8,128)} fusion(f32[2048,128]{1,0:T(8,128)S(1)} %copy-done.1, s32[4096]{0:T(1024)S(1)} %fusion.30), kind=kCustom, calls=%fused_computation | custom fusion | bytes 4210688 | tf_op jit(solution)/shard_map/jit(_take)/gather | solution.py:26
  41.9 2.9 broadcast_select_fusion
  44.8 5.9 all-to-all-start.1
  50.7 0.0 copy-done.6
  50.7 2.0 copy.23
  52.7 3.2 reshape.150
  55.9 2.0 copy.21
  57.9 3.2 reshape.161
  61.1 3.3 reshape.147
  64.5 0.1 compare_select_fusion
  64.5 34.9 %all-to-all-done.1 = f32[32,128,128]{2,1,0:T(8,128)} async-done(((f32[32,128,128]{2,1,0:T(8,128)}), f32[32,128,128]{2,1,0:T(8,128)}, u32[]{:S(2)}, u32[]{:S(2)}) %all-to-all-start.1) | async-done | bytes 2097184 | tf_op jit(solution)/shard_map/all_to_all | solution.py:25
  99.4 56.1 %gather_fusion.1 = f32[16384,128]{1,0:T(8,128)} fusion(f32[4096,128]{1,0:T(8,128)} %bitcast.5, s32[16384]{0:T(1024)S(1)} %broadcast_clamp_fusion), kind=kCustom, calls=%fused_computation.1 | custom fusion | bytes 16842752 | tf_op jit(solution)/shard_map/gather | solution.py:32
  155.5 8.0 %multiply_reduce_fusion = bf16[512,8,128]{2,1,0:T(8,128)(2,1)S(1)} fusion(f32[512,8,4,128]{3,2,1,0:T(4,128)} %bitcast.48, f32[512,8,4]{2,1,0:T(8,128)} %fusion.4), kind=kLoop, calls=%fused_computation.6 | loop fusion | flops 3670016 | bytes 9502720 | tf_op jit(solution)/shard_map/reduce_sum | solution.py:33
  163.5 0.0 copy-done
  163.5 0.0 copy-done.8
  163.5 0.0 copy-start.7
  163.5 0.0 copy-start.9
  163.6 0.0 copy-start.10
  163.6 0.0 copy-start.11
  163.6 1.4 fusion.3
  164.9 0.0 copy-start.14
  165.0 0.0 copy-done.7
  165.0 0.0 copy-done.9
  165.0 0.0 copy-done.10
  165.0 0.0 copy-done.11
  165.0 1.0 fusion.33
  166.0 0.0 copy-done.14
  166.0 0.0 copy-start.12
  166.0 1.1 fusion.5
  167.1 0.0 copy-done.12
  167.1 0.0 copy-start.2
  167.1 1.3 add_bitcast_fusion
  168.4 0.0 copy-done.2
  168.5 1.8 copy.25
  170.2 7.4 %mul.73 = f32[512,8,4,128]{3,2,1,0:T(4,128)} broadcast(f32[512,8,128]{2,1,0:T(8,128)} %bitcast.54), dimensions={0,1,3} | broadcast | bytes 10485760 | tf_op jit(solution)/shard_map/mul | solution.py:53
  177.6 97.5 %scatter_custom_fusion = f32[4096,128]{1,0:T(8,128)} fusion(s32[16384]{0:T(1024)S(1)} %bitcast.59, f32[16384,128]{1,0:T(8,128)} %bitcast.49, f32[16384]{0:T(1024)S(1)} %reshape.150, f32[]{:T(128)} %constant.12.clone.1), kind=kCustom, calls=%fused_computation.4 | custom fusion | flops 4194304 | bytes 10551300 | tf_op jit(solution)/shard_map/scatter-add | solution.py:55
  275.1 6.4 all-to-all-start.2
  281.6 0.0 all-reduce.7.cloned.1.call-start
  281.6 0.0 copy-start.3
  281.6 4.0 fusion.21
  285.6 3.3 fusion.8
  288.9 0.0 all-reduce.7.cloned.1.call-update
  288.9 0.0 copy-start.13
  288.9 0.0 all-reduce.5.cloned.1.call-start
  289.0 46.8 %all-to-all-done.2 = f32[32,128,128]{2,1,0:T(8,128)} async-done(((f32[32,128,128]{2,1,0:T(8,128)}), f32[32,128,128]{2,1,0:T(8,128)}, u32[]{:S(2)}, u32[]{:S(2)}) %all-to-all-start.2) | async-done | bytes 2097184 | tf_op jit(solution)/shard_map/all_to_all | solution.py:57
  335.8 23.9 %scatter_custom_fusion.1 = f32[2048,128]{1,0:T(8,128)} fusion(s32[4096]{0:T(1024)S(1)} %bitcast.61, f32[4096,128]{1,0:T(8,128)} %bitcast.16, f32[]{:T(128)} %constant.12.clone.1), kind=kCustom, calls=%fused_computation.30 | custom fusion | flops 524288 | bytes 1049088 | tf_op jit(solution)/shard_map/scatter-add | solution.py:61
  359.7 0.0 all-reduce.5.cloned.1.call-update
  359.7 0.9 fusion.25
  360.6 73.6 %all-reduce = (f32[1024]{0:T(1024)}, f32[512]{0:T(512)}, f32[512]{0:T(512)}) all-reduce(f32[1024]{0:T(1024)S(1)} %get-tuple-element.14, f32[512]{0:T(512)S(1)} %get-tuple-element.16, f32[512]{0:T(512)S(1)} %bitcast.62), channel_id=1, replica_groups=mesh['dp'=8,'shard'=32] {'dp','shard'}, use_global_device_ids=true, to_apply=%region_4.5 | all-reduce | flops 2048 | bytes 16384 | tf_op jit(solution)/shard_map/psum | solution.py:64
  434.2 1.8 fusion.27
  436.0 140.7 %all-reduce.7.cloned.1.call-done = (f32[1024,1024]{1,0:T(8,128)}, f32[1024,512]{1,0:T(8,128)}) async-done(((f32[1024,1024]{1,0:T(8,128)}, f32[1024,512]{1,0:T(8,128)}), (f32[1024,1024]{1,0:T(8,128)}, f32[1024,512]{1,0:T(8,128)})) %all-reduce.7.cloned.1.call-update) | async-done | bytes 6291472 | tf_op jit(solution)/shard_map/psum | solution.py:64
  576.7 69.3 %all-reduce.5.cloned.1.call-done = f32[2048,128]{1,0:T(8,128)} async-done(((f32[2048,128]{1,0:T(8,128)}), f32[2048,128]{1,0:T(8,128)}) %all-reduce.5.cloned.1.call-update) | async-done | bytes 1048592 | tf_op jit(solution)/shard_map/psum | solution.py:63
  646.0 4.9 copy.47
  651.0 0.0 copy-done.4
  651.0 1.3 copy.48
  652.3 0.6 copy-done.5
  652.9 1.0 copy.49
  (11 shorter events, 0.1 us)
Async XLA Ops:
  7.2 156.3 %copy-start = (bf16[1024,1024]{1,0:T(8,128)(2,1)S(1)}, bf16[1024,1024]{1,0:T(8,128)(2,1)}, u32[]{:S(2)}) copy-start(bf16[1024,1024]{1,0:T(8,128)(2,1)} %param.11) | copy-start | bytes 6291460
  7.2 20.5 %copy-start.1 = (f32[2048,128]{1,0:T(8,128)S(1)}, f32[2048,128]{1,0:T(8,128)}, u32[]{:S(2)}) copy-start(f32[2048,128]{1,0:T(8,128)} %param.10) | copy-start | bytes 3145732
  7.2 20.4 %all-to-all-start = ((s32[32,1,128]{2,1,0:T(1,128)}), s32[32,1,128]{2,1,0:T(1,128)S(1)}, u32[]{:S(2)}, u32[]{:S(2)}) async-start(s32[32,1,128]{2,1,0:T(1,128)} %bitcast.60), calls=%async_computation | async-start | bytes 32768 | tf_op jit(solution)/shard_map/all_to_all | solution.py:24
  44.8 5.9 copy-start.6
  44.8 54.6 %all-to-all-start.1 = ((f32[32,128,128]{2,1,0:T(8,128)}), f32[32,128,128]{2,1,0:T(8,128)}, u32[]{:S(2)}, u32[]{:S(2)}) async-start(f32[32,128,128]{2,1,0:T(8,128)} %broadcast_select_fusion), calls=%async_computation.1 | async-start | bytes 4194304 | tf_op jit(solution)/shard_map/all_to_all | solution.py:25
  155.5 8.1 %copy-start.8 = (f32[1024]{0:T(1024)S(1)}, f32[1024]{0:T(1024)}, u32[]{:S(2)}) copy-start(f32[1024]{0:T(1024)} %param.12) | copy-start | bytes 12292
  163.5 1.4 copy-start.7
  163.5 1.4 copy-start.9
  163.6 1.4 copy-start.10
  163.6 1.4 copy-start.11
  164.9 1.1 copy-start.14
  166.0 1.1 copy-start.12
  167.1 1.3 copy-start.2
  275.1 60.7 %all-to-all-start.2 = ((f32[32,128,128]{2,1,0:T(8,128)}), f32[32,128,128]{2,1,0:T(8,128)}, u32[]{:S(2)}, u32[]{:S(2)}) async-start(f32[32,128,128]{2,1,0:T(8,128)} %bitcast.55), calls=%async_computation.2 | async-start | bytes 4194304 | tf_op jit(solution)/shard_map/all_to_all | solution.py:57
  281.6 295.2 %all-reduce.7.cloned.1.call-start = ((), (), s32[]{:S(2)}) async-start(), calls=%async_computation.4 | async-start | bytes 12582912 | tf_op jit(solution)/shard_map/psum | solution.py:64
  281.6 4.0 copy-start.3
  288.9 70.8 %copy-start.13 = (f32[512,512]{1,0:T(8,128)S(1)}, f32[512,512]{1,0:T(8,128)}, u32[]{:S(2)}) copy-start(f32[512,512]{1,0:T(8,128)} %copy-done.12) | copy-start | bytes 3145732
  288.9 357.1 %all-reduce.5.cloned.1.call-start = ((), (), s32[]{:S(2)}) async-start(), calls=%async_computation.3 | async-start | bytes 2097152 | tf_op jit(solution)/shard_map/psum | solution.py:63
  646.0 4.9 copy-start.4
  651.0 2.0 copy-start.5
Sparse Core Ops, SparseCore 0:
  289.1 287.6 all-reduce.6
  579.8 66.2 all-reduce.4
where the time goes:
time: 661 us
  waiting for transfers between devices  297 us (45%)
  other arithmetic  135 us (20%)
  local copies, waits for them, and re-layouts  102 us (15%)
  blocking collectives  73.6 us (11%)
  starting transfers between devices  24.4 us (4%)
  matrix products  14.7 us (2%)
  between operations  14.4 us (2%)
    psum x1, waiting for transfers between devices, on_device(): lax.psum((g_cross, g_top, g_cbias, g_tbias, g_out), ('dp', 'shard'))  141 us
    scatter-add x1, other arithmetic, on_device(): jnp.zeros(cache_flat.shape, jnp.float32).at[slots.reshape(-1)]  97.5 us
    psum x1, blocking collectives, on_device(): lax.psum((g_cross, g_top, g_cbias, g_tbias, g_out), ('dp', 'shard'))  73.6 us
    psum x1, waiting for transfers between devices, on_device(): table_grad = lax.psum(owner_grad, 'dp')  69.3 us
    gather x1, local copies, waits for them, and re-layouts, on_device(): gathered = cache_flat[slots]  56.1 us
    all_to_all x1, waiting for transfers between devices, on_device(): lax.all_to_all(slot_grads.reshape(cache.shape), 'shard', split_axis=0, co...  46.8 us
    all_to_all x1, waiting for transfers between devices, on_device(): lax.all_to_all(jnp.take(table, served, axis=0), 'shard', split_axis=0, co...  34.9 us
    scatter-add x1, other arithmetic, on_device(): jnp.zeros(table.shape, jnp.float32).at[served.reshape(-1)]  23.9 us
  transfers between devices with their start and end apart: 5, of which 5 were waited for; matrix products, arithmetic and copies ran while one was open for 8% of the time, Pallas kernels for 0%

commit v1 on v0

--- a/solution.py
+++ b/solution.py
@@ -61,7 +61,7 @@
         jnp.zeros(table.shape, jnp.float32).at[served.reshape(-1)].add(returned.reshape(-1, emb))
     )
     table_grad = lax.psum(owner_grad, "dp")
-    summed = lax.psum((g_cross, g_top, g_cbias, g_tbias, g_out), ("dp", "shard"))
+    summed = lax.psum(lax.psum((g_cross, g_top, g_cbias, g_tbias, g_out), "shard"), "dp")
     return (logits, summed[0], summed[1], summed[2], summed[3], summed[4], table_grad)
 
 

time: 661 us -> 502 us (0.76)
  waiting for transfers between devices: 297 us -> 112 us
  blocking collectives: 73.6 us -> 105 us
  starting transfers between devices: 24.4 us -> 12.4 us
    psum x2, waiting for transfers between devices: 210 us -> 15 us  [the longest x1 13.1 us: on_device(): lax.psum(lax.psum((g_cross, g_top, g_cbias, g_tbias, g_out), 'shard'), 'dp')]
    all_to_all x0 -> x1, blocking collectives: none -> 20.3 us  [on_device(): lax.all_to_all(requests, 'shard', split_axis=0, concat_axis=0, tiled=True)]
    all_to_all x1, waiting for transfers between devices: 46.8 us -> 61.5 us  [on_device(): lax.all_to_all(slot_grads.reshape(cache.shape), 'shard', split_axis=0, co...]
    all_to_all x1 -> x0, starting transfers between devices: 12 us -> none  [on_device(): lax.all_to_all(requests, 'shard', split_axis=0, concat_axis=0, tiled=True)]
    psum x1 -> x2, blocking collectives: 73.6 us -> 84.8 us  [the longest x1 71.3 us: on_device(): lax.psum((g_cross, g_top, g_cbias, g_tbias, g_out), 'shard')]
    unnamed x36 -> x32, local copies, waits for them, and re-layouts: 12.6 us -> 14.4 us
  transfers between devices with their start and end apart: 5 -> 4, of which waited for: 5 -> 4; matrix products, arithmetic and copies ran while one was open for 8% -> 31% of each run, Pallas kernels for 0% -> 0%
where the time goes in v1:
time: 502 us; the launch traced here: 501 us
  other arithmetic  135 us (27%)
  waiting for transfers between devices  112 us (22%)
  local copies, waits for them, and re-layouts  105 us (21%)
  blocking collectives  105 us (21%)
  matrix products  17.2 us (3%)
  between operations  14.2 us (3%)
  starting transfers between devices  12.4 us (2%)
    scatter-add x1, other arithmetic, on_device(): jnp.zeros(cache_flat.shape, jnp.float32).at[slots.reshape(-1)]  97.7 us
    psum x1, blocking collectives, on_device(): lax.psum((g_cross, g_top, g_cbias, g_tbias, g_out), 'shard')  71.3 us
    all_to_all x1, waiting for transfers between devices, on_device(): lax.all_to_all(slot_grads.reshape(cache.shape), 'shard', split_axis=0, co...  61.5 us
    gather x1, local copies, waits for them, and re-layouts, on_device(): gathered = cache_flat[slots]  56.1 us
    all_to_all x1, waiting for transfers between devices, on_device(): lax.all_to_all(jnp.take(table, served, axis=0), 'shard', split_axis=0, co...  35.2 us
    scatter-add x1, other arithmetic, on_device(): jnp.zeros(table.shape, jnp.float32).at[served.reshape(-1)]  23.6 us
    all_to_all x1, blocking collectives, on_device(): lax.all_to_all(requests, 'shard', split_axis=0, concat_axis=0, tiled=True)  20.3 us
    gather x1, local copies, waits for them, and re-layouts, on_device(): jnp.take(table, served, axis=0)  15.4 us
  transfers between devices with their start and end apart: 4, of which 4 were waited for; matrix products, arithmetic and copies ran while one was open for 31% of the time, Pallas kernels for 0%

profile of v1, /device:TPU:8, one launch (start us, length us, event | category | flops | bytes accessed | tf_op | source)
XLA Modules:
  0.0 500.6 jit_solution(799716004464130457)
XLA Ops:
  7.2 0.0 copy-start
  7.2 20.3 %all_to_all.25 = s32[32,1,128]{2,1,0:T(1,128)S(1)} all-to-all(s32[32,1,128]{2,1,0:T(1,128)} %bitcast.60), channel_id=1, replica_groups=mesh['dp'=8,'shard'=32] {'shard'}, dimensions={0} | all-to-all | bytes 32768 | tf_op jit(solution)/shard_map/all_to_all | solution.py:24
  27.5 15.4 %gather_fusion = f32[4096,128]{1,0:T(8,128)} fusion(f32[2048,128]{1,0:T(8,128)} %param.10, s32[4096]{0:T(1024)S(1)} %fusion.30), kind=kCustom, calls=%fused_computation | custom fusion | bytes 4210688 | tf_op jit(solution)/shard_map/jit(_take)/gather | solution.py:26
  42.9 2.9 broadcast_select_fusion
  45.8 0.0 copy-start.5
  45.8 0.0 copy-start.4
  45.8 5.9 %all-to-all-start.1 = ((f32[32,128,128]{2,1,0:T(8,128)}), f32[32,128,128]{2,1,0:T(8,128)}, u32[]{:S(2)}, u32[]{:S(2)}) async-start(f32[32,128,128]{2,1,0:T(8,128)} %broadcast_select_fusion), calls=%async_computation.1 | async-start | bytes 4194304 | tf_op jit(solution)/shard_map/all_to_all | solution.py:25
  51.7 0.0 all-reduce.7.cloned.1.call-start
  51.8 0.0 copy-done.5
  51.8 0.1 copy.22
  51.9 0.0 copy-done.4
  51.9 2.0 copy.23
  54.0 2.0 copy.21
  56.0 3.2 reshape.161
  59.2 3.3 reshape.147
  62.5 2.8 fusion.4
  65.3 35.2 %all-to-all-done.1 = f32[32,128,128]{2,1,0:T(8,128)} async-done(((f32[32,128,128]{2,1,0:T(8,128)}), f32[32,128,128]{2,1,0:T(8,128)}, u32[]{:S(2)}, u32[]{:S(2)}) %all-to-all-start.1) | async-done | bytes 2097184 | tf_op jit(solution)/shard_map/all_to_all | solution.py:25
  100.4 56.1 %gather_fusion.1 = f32[16384,128]{1,0:T(8,128)} fusion(f32[4096,128]{1,0:T(8,128)} %bitcast.5, s32[16384]{0:T(1024)S(1)} %broadcast_clamp_fusion), kind=kCustom, calls=%fused_computation.1 | custom fusion | bytes 16842752 | tf_op jit(solution)/shard_map/gather | solution.py:32
  156.5 0.0 copy-start.7
  156.5 7.9 %multiply_reduce_fusion = bf16[512,8,128]{2,1,0:T(8,128)(2,1)S(1)} fusion(f32[512,8,4,128]{3,2,1,0:T(4,128)} %bitcast.48, f32[512,8,4]{2,1,0:T(8,128)} %fusion.4), kind=kLoop, calls=%fused_computation.6 | loop fusion | flops 3670016 | bytes 9502720 | tf_op jit(solution)/shard_map/reduce_sum | solution.py:33
  164.4 0.0 copy-done
  164.4 0.0 copy-done.7
  164.4 0.0 copy-start.6
  164.4 0.0 copy-start.8
  164.4 0.0 copy-start.9
  164.4 0.0 copy-start.10
  164.5 2.7 fusion.3
  167.1 0.0 copy-done.6
  167.1 0.0 copy-done.8
  167.1 0.0 copy-done.9
  167.1 0.0 copy-done.10
  167.1 1.0 fusion.33
  168.1 0.0 copy-start.11
  168.2 2.3 fusion.21
  170.5 0.0 copy-done.11
  170.5 1.1 fusion.5
  171.6 0.0 copy-start.1
  171.6 1.3 copy-done.1
  172.9 3.3 fusion.8
  176.2 0.0 all-reduce.7.cloned.1.call-update
  176.3 0.1 compare_select_fusion
  176.3 3.2 reshape.150
  179.6 4.2 add_bitcast_fusion
  183.7 1.8 copy.25
  185.5 7.4 %mul.73 = f32[512,8,4,128]{3,2,1,0:T(4,128)} broadcast(f32[512,8,128]{2,1,0:T(8,128)} %bitcast.54), dimensions={0,1,3} | broadcast | bytes 10485760 | tf_op jit(solution)/shard_map/mul | solution.py:53
  192.9 97.7 %scatter_custom_fusion = f32[4096,128]{1,0:T(8,128)} fusion(s32[16384]{0:T(1024)S(1)} %bitcast.59, f32[16384,128]{1,0:T(8,128)} %bitcast.49, f32[16384]{0:T(1024)S(1)} %reshape.150, f32[]{:T(128)} %constant.12.clone.1), kind=kCustom, calls=%fused_computation.4 | custom fusion | flops 4194304 | bytes 10551300 | tf_op jit(solution)/shard_map/scatter-add | solution.py:55
  290.6 6.4 %all-to-all-start.2 = ((f32[32,128,128]{2,1,0:T(8,128)}), f32[32,128,128]{2,1,0:T(8,128)}, u32[]{:S(2)}, u32[]{:S(2)}) async-start(f32[32,128,128]{2,1,0:T(8,128)} %bitcast.55), calls=%async_computation.2 | async-start | bytes 4194304 | tf_op jit(solution)/shard_map/all_to_all | solution.py:57
  297.0 0.0 all-reduce.9.cloned.1.call-start
  297.1 61.5 %all-to-all-done.2 = f32[32,128,128]{2,1,0:T(8,128)} async-done(((f32[32,128,128]{2,1,0:T(8,128)}), f32[32,128,128]{2,1,0:T(8,128)}, u32[]{:S(2)}, u32[]{:S(2)}) %all-to-all-start.2) | async-done | bytes 2097184 | tf_op jit(solution)/shard_map/all_to_all | solution.py:57
  358.6 23.6 %scatter_custom_fusion.1 = f32[2048,128]{1,0:T(8,128)} fusion(s32[4096]{0:T(1024)S(1)} %bitcast.61, f32[4096,128]{1,0:T(8,128)} %bitcast.16, f32[]{:T(128)} %constant.12.clone.1), kind=kCustom, calls=%fused_computation.30 | custom fusion | flops 524288 | bytes 1049088 | tf_op jit(solution)/shard_map/scatter-add | solution.py:61
  382.2 1.8 all-reduce.7.cloned.1.call-done
  384.0 0.0 copy-start.12
  384.0 0.0 all-reduce.9.cloned.1.call-update
  384.1 1.2 copy-done.12
  385.3 0.9 fusion.25
  386.1 71.3 %all-reduce = (f32[1024]{0:T(1024)S(1)}, f32[512]{0:T(512)S(1)}, f32[512]{0:T(512)S(1)}) all-reduce(f32[1024]{0:T(1024)S(1)} %get-tuple-element.20, f32[512]{0:T(512)S(1)} %get-tuple-element.22, f32[512]{0:T(512)S(1)} %bitcast.62), channel_id=1, replica_groups=mesh['dp'=8,'shard'=32] {'shard'}, use_global_device_ids=true, to_apply=%region_6.7 | all-reduce | flops 2048 | bytes 16384 | tf_op jit(solution)/shard_map/psum | solution.py:64
  457.5 13.5 %all-reduce.2 = (f32[1024]{0:T(1024)}, f32[512]{0:T(512)}, f32[512]{0:T(512)}) all-reduce(f32[1024]{0:T(1024)S(1)} %get-tuple-element.7, f32[512]{0:T(512)S(1)} %get-tuple-element.8, f32[512]{0:T(512)S(1)} %get-tuple-element.9), channel_id=1, replica_groups=mesh['dp'=8,'shard'=32] {'dp'}, use_global_device_ids=true, to_apply=%region_7.8 | all-reduce | flops 2048 | bytes 16384 | tf_op jit(solution)/shard_map/psum | solution.py:64
  471.0 1.8 fusion.27
  472.8 13.1 %all-reduce.9.cloned.1.call-done = (f32[1024,1024]{1,0:T(8,128)}, f32[1024,512]{1,0:T(8,128)}, f32[2048,128]{1,0:T(8,128)}) async-done(((f32[1024,1024]{1,0:T(8,128)}, f32[1024,512]{1,0:T(8,128)}, f32[2048,128]{1,0:T(8,128)}), (f32[1024,1024]{1,0:T(8,128)}, f32[1024,512]{1,0:T(8,128)}, f32[2048,128]{1,0:T(8,128)})) %all-reduce.9.cloned.1.call-update) | async-done | bytes 7340048 | tf_op jit(solution)/shard_map/psum | solution.py:64
  485.9 4.9 copy.49
  490.8 0.0 copy-done.2
  490.8 1.3 copy.50
  492.1 0.6 copy-done.3
  492.8 1.0 copy.51
  (7 shorter events, 0.1 us)
Async XLA Ops:
  7.2 157.2 %copy-start = (bf16[1024,1024]{1,0:T(8,128)(2,1)S(1)}, bf16[1024,1024]{1,0:T(8,128)(2,1)}, u32[]{:S(2)}) copy-start(bf16[1024,1024]{1,0:T(8,128)(2,1)} %param.11) | copy-start | bytes 6291460
  45.8 6.0 %copy-start.5 = (s32[512,8]{0,1:T(8,128)S(1)}, s32[512,8]{0,1:T(8,128)}, u32[]{:S(2)}) copy-start(s32[512,8]{0,1:T(8,128)} %param.18) | copy-start | bytes 49156
  45.8 6.1 %copy-start.4 = (s32[512,8,4]{0,2,1:T(4,128)S(1)}, s32[512,8,4]{0,2,1:T(4,128)}, u32[]{:S(2)}) copy-start(s32[512,8,4]{0,2,1:T(4,128)} %param.17) | copy-start | bytes 196612
  45.8 54.6 %all-to-all-start.1 = ((f32[32,128,128]{2,1,0:T(8,128)}), f32[32,128,128]{2,1,0:T(8,128)}, u32[]{:S(2)}, u32[]{:S(2)}) async-start(f32[32,128,128]{2,1,0:T(8,128)} %broadcast_select_fusion), calls=%async_computation.1 | async-start | bytes 4194304 | tf_op jit(solution)/shard_map/all_to_all | solution.py:25
  51.7 332.3 %all-reduce.7.cloned.1.call-start = ((), (), s32[]{:S(2)}) async-start(), calls=%async_computation.3 | async-start | bytes 12582912 | tf_op jit(solution)/shard_map/psum | solution.py:64
  156.5 7.9 %copy-start.7 = (f32[1024]{0:T(1024)S(1)}, f32[1024]{0:T(1024)}, u32[]{:S(2)}) copy-start(f32[1024]{0:T(1024)} %param.12) | copy-start | bytes 12292
  164.4 2.7 copy-start.6
  164.4 2.7 copy-start.8
  164.4 2.7 copy-start.9
  164.4 2.7 copy-start.10
  168.1 2.3 copy-start.11
  171.6 1.3 copy-start.1
  290.6 68.0 %all-to-all-start.2 = ((f32[32,128,128]{2,1,0:T(8,128)}), f32[32,128,128]{2,1,0:T(8,128)}, u32[]{:S(2)}, u32[]{:S(2)}) async-start(f32[32,128,128]{2,1,0:T(8,128)} %bitcast.55), calls=%async_computation.2 | async-start | bytes 4194304 | tf_op jit(solution)/shard_map/all_to_all | solution.py:57
  297.0 188.9 %all-reduce.9.cloned.1.call-start = ((), (), s32[]{:S(2)}) async-start(), calls=%async_computation.4 | async-start | bytes 14680064 | tf_op jit(solution)/shard_map/psum | solution.py:64
  384.0 1.2 copy-start.12
  485.9 4.9 copy-start.2
  490.8 2.0 copy-start.3
Sparse Core Ops, SparseCore 0:
  176.4 207.6 all-reduce.6
  387.3 98.5 all-reduce.8
